TPU v7x, 32 devices: a whole 2x2x4 slice. The times are simulated.
32 devices in a mesh: ctx: 8 (over z, x), ch: 4 (over y, core).
Axes of the slice: x: 2, y: 2, z: 4, core: 2. Of those that a mesh axis runs over, the one named last changes fastest.
Arguments:
- signal: float32 [64, 65536], P('ch', 'ctx'), parts along dimension 0, may hold values from -6 to 6
- gate: float32 [64, 65536], P('ch', 'ctx'), parts along dimension 0, may hold values from -6 to 6
- skip: float32 [64], P('ch'), parts along dimension 0, may hold values from 0.5 to 1.5
- filter_spectrum: float32 [16, 2, 64, 8192], P('ctx', None, 'ch'), parts along dimension 2, may hold values from -6 to 6
Outputs:
- gated: float32 [64, 65536], P('ch', 'ctx'), parts along dimension 0
There are 4 independent parts, one for each index of `ch`. A program takes and returns all parts, laid end to end along the dimension named above; each array names one. Nothing has to cross between parts.
All inputs are finite; a program needn't handle non-finite values.
Results may differ from a plain program's by a relative error of at most 0.00005.
Values sent between devices are 32-bit elements; how exact they have to be, the bound alone decides.
No kernel may reach another device: no remote copies, remote signals or barrier semaphores. Data moves between devices by JAX's collectives and lax.ppermute only.
A program may use at most 128 MiB of HBM per device.

v0:
```python
import math
import jax
import jax.numpy as jnp
from jax import lax
from jax.sharding import PartitionSpec as P


def contract(form, left, right):
    return jnp.einsum(form, left, right, precision=lax.Precision.HIGHEST)


def phase_table(left, right, period):
    angle = left * right % period
    theta = angle.astype(jnp.float32) * (2.0 * math.pi / period)
    return (jnp.cos(theta), jnp.sin(theta))


def product_pair(form, left, right):
    real_part = contract(form, left[0], right[0]) - contract(form, left[1], right[1])
    imag_part = contract(form, left[0], right[1]) + contract(form, left[1], right[0])
    return (real_part, imag_part)


def times_pair(left, right):
    return (left[0] * right[0] - left[1] * right[1], left[0] * right[1] + left[1] * right[0])


def local_tables(length):
    outer_len = 128
    inner_len = length // outer_len
    outer_index = jnp.arange(outer_len, dtype=jnp.int32)
    inner_index = jnp.arange(inner_len, dtype=jnp.int32)
    outer_wave = phase_table(outer_index[:, None], outer_index[None, :], outer_len)
    twist_wave = phase_table(outer_index[:, None], inner_index[None, :], length)
    inner_wave = phase_table(inner_index[:, None], inner_index[None, :], inner_len)
    return (outer_len, inner_len, outer_wave, twist_wave, inner_wave)


def local_forward(values, length):
    outer_len, inner_len, outer_wave, twist_wave, inner_wave = local_tables(length)
    lead_shape = values[0].shape[:-1]
    values = tuple((part.reshape(lead_shape + (outer_len, inner_len)) for part in values))
    values = product_pair("as,...sb->...ab", (outer_wave[0], -outer_wave[1]), values)
    values = times_pair(values, (twist_wave[0], -twist_wave[1]))
    return product_pair("...as,bs->...ab", values, (inner_wave[0], -inner_wave[1]))


def local_inverse(values, length):
    outer_len, inner_len, outer_wave, twist_wave, inner_wave = local_tables(length)
    lead_shape = values[0].shape[:-2]
    values = product_pair("...ak,sk->...as", values, inner_wave)
    values = times_pair(values, twist_wave)
    values = product_pair("ta,...as->...ts", outer_wave, values)
    return tuple((part.reshape(lead_shape + (length,)) for part in values))


def shards(signal, gate, skip, filter_spectrum):
    parts_count = lax.axis_size("ctx")
    freq_rows = 2 * parts_count
    channels, tok_local = signal.shape
    slice_len = tok_local // parts_count
    full_len = freq_rows * tok_local
    device = lax.axis_index("ctx")
    is_first = device == 0
    columns = lax.all_to_all(signal[None], "ctx", split_axis=2, concat_axis=0, tiled=True)
    source_row = jnp.arange(parts_count, dtype=jnp.int32)
    dest_index = jnp.arange(parts_count, dtype=jnp.int32)
    slice_pos = device * slice_len + jnp.arange(slice_len, dtype=jnp.int32)
    upper_freq = jnp.where(dest_index == 0, parts_count, freq_rows - dest_index)
    row_freq = jnp.stack([dest_index, upper_freq], axis=1).reshape(freq_rows)
    spot = jnp.arange(tok_local, dtype=jnp.int32)
    wave_cos, wave_sin = phase_table(row_freq[:, None], source_row[None, :], freq_rows)
    first_re = contract("kr,rcq->kcq", wave_cos, columns)
    first_im = -contract("kr,rcq->kcq", wave_sin, columns)
    twist_cos, twist_sin = phase_table(row_freq[:, None], slice_pos[None, :], full_len)
    first_pair = times_pair((first_re, first_im), (twist_cos[:, None, :], -twist_sin[:, None, :]))
    stacked = jnp.stack(first_pair, axis=1)
    moved = lax.all_to_all(stacked, "ctx", split_axis=0, concat_axis=3, tiled=True)
    low_pair = (moved[0, 0], moved[0, 1])
    high_pair = (moved[1, 0], moved[1, 1])
    rows_pair = (jnp.stack([low_pair[0], high_pair[0]]), jnp.stack([low_pair[1], high_pair[1]]))
    spectral = local_forward(rows_pair, tok_local)
    inner_len = tok_local // 128
    filt = filter_spectrum.reshape(2, 2, channels, inner_len, 128).swapaxes(3, 4)
    product = times_pair(spectral, (filt[:, 0], filt[:, 1]))
    restored = local_inverse(product, tok_local)
    my_freq = jnp.stack([device, jnp.where(is_first, parts_count, freq_rows - device)])
    back_cos, back_sin = phase_table(my_freq[:, None], spot[None, :], full_len)
    turned = times_pair(restored, (back_cos[:, None, :], back_sin[:, None, :]))
    scale_factor = 1.0 / full_len
    stacked = jnp.stack(turned, axis=1)
    moved = lax.all_to_all(stacked, "ctx", split_axis=3, concat_axis=0, tiled=True)
    out_cos, out_sin = phase_table(source_row[:, None], row_freq[None, :], freq_rows)
    rows_all = contract("rm,mcq->rcq", out_cos, moved[:, 0]) - contract(
        "rm,mcq->rcq", out_sin, moved[:, 1]
    )
    rows_all = rows_all * scale_factor
    convolved = lax.all_to_all(rows_all, "ctx", split_axis=0, concat_axis=2, tiled=True)
    return gate * (convolved[0] + skip[:, None] * signal)


def solution(mesh):
    return jax.shard_map(
        shards,
        mesh=mesh,
        in_specs=(P("ch", "ctx"), P("ch", "ctx"), P("ch"), P("ctx", None, "ch", None)),
        out_specs=P("ch", "ctx"),
        check_vma=False,
    )
```

profile of v0, /device:TPU:0, one launch (start us, length us, event | category | flops | bytes accessed | tf_op | source)
XLA Modules:
  0.0 351.3 jit_solution(4517637440117171831)
XLA Ops:
  0.0 3.5 copy.33
  3.5 0.5 broadcast.483
  4.0 38.3 %reduce = f32[8192,16]{1,0:T(8,128)} reduce(f32[8192,1,16]{2,1,0:T(1,128)} %bitcast.158, f32[]{:T(128)} %broadcast.483), dimensions={1}, to_apply=%bitcast.139.reduce_sub_computation | reduce | bytes 1048580
  42.3 4.4 %reshape.260 = f32[8,1,16384]{2,1,0:T(1,128)} reshape(f32[8192,16]{1,0:T(8,128)} %reduce) | data formatting | bytes 1048576
  46.7 7.8 %all-to-all-start = ((f32[8,1,16384]{2,1,0:T(1,128)}), f32[8,1,16384]{2,1,0:T(1,128)S(1)}, u32[]{:S(2)}, u32[]{:S(2)}) async-start(f32[8,1,16384]{2,1,0:T(1,128)} %reshape.260), calls=%async_computation | async-start | bytes 1048576 | tf_op jit(solution)/shard_map/all_to_all | solution.py:65
  54.7 0.3 fusion.69
  55.1 13.9 %all-to-all-done = f32[8,1,16384]{2,1,0:T(1,128)S(1)} async-done(((f32[8,1,16384]{2,1,0:T(1,128)}), f32[8,1,16384]{2,1,0:T(1,128)S(1)}, u32[]{:S(2)}, u32[]{:S(2)}) %all-to-all-start) | async-done | bytes 524320 | tf_op jit(solution)/shard_map/all_to_all | solution.py:65
  68.9 1.8 reduce.1
  70.7 10.2 %reshape.261 = f32[8192,1,16]{2,1,0:T(1,128)} reshape(f32[8,16384]{1,0:T(8,128)S(1)} %reduce.1) | data formatting | bytes 1048576
  80.9 2.9 copy.55
  83.8 1.1 convolution_negate_fusion
  84.9 1.3 subtract_bitcast_fusion
  86.4 2.5 copy.35
  89.0 3.6 %all-to-all-start.1 = ((f32[16,2,16,1024]{3,2,1,0:T(8,128)}), f32[16,2,16,1024]{3,2,1,0:T(8,128)S(1)}, u32[]{:S(2)}, u32[]{:S(2)}) async-start(f32[16,2,16,1024]{3,2,1,0:T(8,128)} %copy.35), calls=%async_computation.1 | async-start | bytes 4194304 | tf_op jit(solution)/shard_map/all_to_all | solution.py:78
  92.6 2.0 copy.58
  94.6 1.5 copy.63
  96.5 1.2 fusion.54
  97.7 43.4 %all-to-all-done.1 = f32[16,2,16,1024]{3,2,1,0:T(8,128)S(1)} async-done(((f32[16,2,16,1024]{3,2,1,0:T(8,128)}), f32[16,2,16,1024]{3,2,1,0:T(8,128)S(1)}, u32[]{:S(2)}, u32[]{:S(2)}) %all-to-all-start.1) | async-done | bytes 2097184 | tf_op jit(solution)/shard_map/all_to_all | solution.py:78
  141.0 2.5 copy.64
  143.6 1.9 all_to_all.57
  145.5 1.1 fusion.195
  146.6 1.5 stack.46
  148.1 0.3 copy.37
  148.4 0.4 stack.50
  148.8 0.3 copy.40
  149.2 0.4 stack.49
  149.6 0.3 copy.39
  149.9 1.5 stack.47
  151.4 0.3 copy.38
  151.7 1.2 fusion.6
  152.9 1.2 fusion.7
  154.2 1.2 fusion.2
  155.4 1.3 fusion.3
  156.7 1.3 fusion.11
  158.0 1.3 fusion.12
  159.3 1.3 convolution_subtract_fusion.2
  160.7 0.3 copy-done
  160.9 2.1 multiply_add_fusion.2
  163.0 1.2 fusion.43
  164.2 1.2 fusion.47
  165.4 1.2 convolution_add_fusion.1
  166.5 1.2 convolution_subtract_fusion.1
  167.7 1.2 fusion.14
  169.0 2.2 fusion.13
  171.2 1.2 fusion
  172.4 2.0 copy.43
  174.4 2.1 reshape.248
  176.5 3.5 fusion.1
  180.0 1.8 copy.42
  181.8 1.6 reshape.247
  183.5 1.4 multiply_subtract_fusion
  185.1 15.4 %copy.44 = f32[2,2,16,8192]{2,0,1,3:T(2,128)} copy(f32[2,2,16,8192]{3,2,0,1:T(8,128)S(1)} %pad_maximum_fusion.1) | data formatting | bytes 4194304 | tf_op jit(solution)/shard_map/stack | solution.py:91
  200.4 24.0 %reshape.262 = f32[8,1,65536]{2,1,0:T(1,128)S(1)} reshape(f32[8192,2,2,16]{3,2,1,0:T(2,128)} %bitcast.155) | data formatting | bytes 4194304
  224.5 51.9 %all_to_all.69 = f32[8,1,65536]{2,1,0:T(1,128)} all-to-all(f32[8,1,65536]{2,1,0:T(1,128)S(1)} %reshape.262), channel_id=1, replica_groups=mesh['ctx'=8,'ch'=4] {'ctx'}, dimensions={0} | all-to-all | bytes 4194304 | tf_op jit(solution)/shard_map/all_to_all | solution.py:92
  276.4 7.1 %reduce.2 = f32[8,65536]{1,0:T(8,128)S(1)} reduce(f32[8,1,65536]{2,1,0:T(1,128)} %all_to_all.69, f32[]{:T(128)} %broadcast.483), dimensions={1}, to_apply=%all_to_all.58.reduce_sub_computation | reduce | bytes 4194308 | tf_op jit(solution)/shard_map/all_to_all | solution.py:92
  283.5 28.4 %reshape.263 = f32[8192,2,2,16]{3,2,1,0:T(2,128)} reshape(f32[8,65536]{1,0:T(8,128)S(1)} %reduce.2) | data formatting | bytes 4194304
  312.0 13.2 %copy.57 = f32[2,2,16,8,1024]{4,3,2,1,0:T(8,128)S(1)} copy(f32[2,2,16,8,1024]{2,0,1,4,3:T(2,128)} %bitcast.156) | data formatting | bytes 4194304 | tf_op jit(solution)/shard_map/all_to_all | solution.py:92
  325.2 3.0 copy.46
  328.2 2.7 all_to_all.61
  330.9 0.6 fusion.5
  331.5 0.6 fusion.4
  332.2 0.3 copy.47
  332.5 17.6 %all_to_all.70 = f32[8,16,1024]{2,1,0:T(8,128)S(1)} all-to-all(f32[8,16,1024]{2,1,0:T(8,128)S(1)} %copy.47), channel_id=1, replica_groups=mesh['ctx'=8,'ch'=4] {'ctx'}, dimensions={0} | all-to-all | bytes 1048576 | tf_op jit(solution)/shard_map/all_to_all | solution.py:98
  350.2 0.9 add_multiply_fusion
  (19 shorter events, 1.0 us)
Async XLA Ops:
  46.7 22.2 %all-to-all-start = ((f32[8,1,16384]{2,1,0:T(1,128)}), f32[8,1,16384]{2,1,0:T(1,128)S(1)}, u32[]{:S(2)}, u32[]{:S(2)}) async-start(f32[8,1,16384]{2,1,0:T(1,128)} %reshape.260), calls=%async_computation | async-start | bytes 1048576 | tf_op jit(solution)/shard_map/all_to_all | solution.py:65
  89.0 52.1 %all-to-all-start.1 = ((f32[16,2,16,1024]{3,2,1,0:T(8,128)}), f32[16,2,16,1024]{3,2,1,0:T(8,128)S(1)}, u32[]{:S(2)}, u32[]{:S(2)}) async-start(f32[16,2,16,1024]{3,2,1,0:T(8,128)} %copy.35), calls=%async_computation.1 | async-start | bytes 4194304 | tf_op jit(solution)/shard_map/all_to_all | solution.py:78
  159.3 1.6 copy-start
  332.2 18.0 %copy-start.1 = (f32[16,8192]{1,0:T(8,128)S(1)}, f32[16,8192]{1,0:T(8,128)}, u32[]{:S(2)}) copy-start(f32[16,8192]{1,0:T(8,128)} %param.4) | copy-start | bytes 1572868
  332.2 18.0 %copy-start.2 = (f32[16,8192]{1,0:T(8,128)S(1)}, f32[16,8192]{1,0:T(8,128)}, u32[]{:S(2)}) copy-start(f32[16,8192]{1,0:T(8,128)} %param.5) | copy-start | bytes 1572868
  332.2 18.0 %copy-start.3 = (f32[16]{0:T(128)S(1)}, f32[16]{0:T(128)}, u32[]{:S(2)}) copy-start(f32[16]{0:T(128)} %param.6) | copy-start | bytes 196
where the time goes:
time: 357 us; the launch traced here: 351 us
  local copies, waits for them, and re-layouts  133 us (37%)
  blocking collectives  69.5 us (19%)
  waiting for transfers between devices  57.2 us (16%)
  other arithmetic  52 us (15%)
  matrix products  27.5 us (8%)
  starting transfers between devices  11.4 us (3%)
    unnamed x16, local copies, waits for them, and re-layouts  73.3 us
    all_to_all x1, blocking collectives, shards(): lax.all_to_all(stacked, 'ctx', split_axis=3, concat_axis=0, tiled=True)  51.9 us
    all_to_all x1, waiting for transfers between devices, shards(): lax.all_to_all(stacked, 'ctx', split_axis=0, concat_axis=3, tiled=True)  43.4 us
    unnamed x1, other arithmetic  38.3 us
    dot_general x20, matrix products, contract(): return jnp.einsum(form, left, right, precision=lax.Precision.HIGHEST)  27.5 us
    all_to_all x3, local copies, waits for them, and re-layouts, shards(): lax.all_to_all(stacked, 'ctx', split_axis=3, concat_axis=0, tiled=True)  18.9 us
    all_to_all x1, blocking collectives, shards(): lax.all_to_all(rows_all, 'ctx', split_axis=0, concat_axis=2, tiled=True)  17.6 us
    another operation x1, local copies, waits for them, and re-layouts, shards(): stacked = jnp.stack(turned, axis=1)  15.4 us
  transfers between devices with their start and end apart: 2, of which 2 were waited for; matrix products, arithmetic and copies ran while one was open for 2% of the time, Pallas kernels for 0%

commit v1 on v0

--- a/solution.py
+++ b/solution.py
@@ -3,6 +3,22 @@
 import jax.numpy as jnp
 from jax import lax
 from jax.sharding import PartitionSpec as P
+
+
+def exchange_in_pairs(shard, axis, split, join):
+    ways, here = (lax.axis_size(axis), lax.axis_index(axis))
+    width = shard.shape[split] // ways
+    lengths = list(shard.shape)
+    lengths[split] = width
+    height = lengths[join]
+    lengths[join] = height * ways
+    full = jnp.zeros(lengths, shard.dtype)
+    for mask in range(ways):
+        part = lax.dynamic_slice_in_dim(shard, (here ^ mask) * width, width, axis=split)
+        if mask:
+            part = lax.ppermute(part, axis, [(d, d ^ mask) for d in range(ways)])
+        full = lax.dynamic_update_slice_in_dim(full, part, (here ^ mask) * height, axis=join)
+    return full
 
 
 def contract(form, left, right):
@@ -75,7 +91,7 @@
     twist_cos, twist_sin = phase_table(row_freq[:, None], slice_pos[None, :], full_len)
     first_pair = times_pair((first_re, first_im), (twist_cos[:, None, :], -twist_sin[:, None, :]))
     stacked = jnp.stack(first_pair, axis=1)
-    moved = lax.all_to_all(stacked, "ctx", split_axis=0, concat_axis=3, tiled=True)
+    moved = exchange_in_pairs(stacked, "ctx", 0, 3)
     low_pair = (moved[0, 0], moved[0, 1])
     high_pair = (moved[1, 0], moved[1, 1])
     rows_pair = (jnp.stack([low_pair[0], high_pair[0]]), jnp.stack([low_pair[1], high_pair[1]]))

time: 357 us -> 357 us (level)
  waiting for transfers between devices: 57.2 us -> 46.3 us
  starting transfers between devices: 11.4 us -> 19.5 us
    all_to_all x1 -> x0, waiting for transfers between devices: 43.4 us -> none  [shards(): lax.all_to_all(stacked, 'ctx', split_axis=0, concat_axis=3, tiled=True)]
    ppermute x0 -> x7, waiting for transfers between devices: none -> 34.8 us  [exchange_in_pairs(): part = lax.ppermute(part, axis, [(d, d ^ mask) for d in range(ways)])]
    ppermute x0 -> x7, starting transfers between devices: none -> 11.7 us  [exchange_in_pairs(): part = lax.ppermute(part, axis, [(d, d ^ mask) for d in range(ways)])]
    another operation x4, local copies, waits for them, and re-layouts: 1.46 us -> 7.72 us  [shards(): jnp.stack([low_pair[1], high_pair[1]])]
    all_to_all x2 -> x0, local copies, waits for them, and re-layouts: 4.45 us -> none  [shards(): lax.all_to_all(stacked, 'ctx', split_axis=0, concat_axis=3, tiled=True)]
    another operation x4, local copies, waits for them, and re-layouts: 3.54 us -> 7.75 us  [shards(): jnp.stack([low_pair[0], high_pair[0]])]
    all_to_all x1 -> x0, starting transfers between devices: 3.64 us -> none  [shards(): lax.all_to_all(stacked, 'ctx', split_axis=0, concat_axis=3, tiled=True)]
    unnamed x16 -> x20, local copies, waits for them, and re-layouts: 73.3 us -> 71.7 us
  transfers between devices with their start and end apart: 2 -> 8, of which waited for: 2 -> 4; matrix products, arithmetic and copies ran while one was open for 2% -> 1% of each run, Pallas kernels for 0% -> 0%
where the time goes in v1:
time: 357 us; the launch traced here: 352 us
  local copies, waits for them, and re-layouts  135 us (38%)
  blocking collectives  68.6 us (19%)
  other arithmetic  53 us (15%)
  waiting for transfers between devices  46.3 us (13%)
  matrix products  28.7 us (8%)
  starting transfers between devices  19.5 us (5%)
    unnamed x20, local copies, waits for them, and re-layouts  71.7 us
    all_to_all x1, blocking collectives, shards(): lax.all_to_all(stacked, 'ctx', split_axis=3, concat_axis=0, tiled=True)  51.2 us
    unnamed x1, other arithmetic  38.4 us
    ppermute x7, waiting for transfers between devices, exchange_in_pairs(): part = lax.ppermute(part, axis, [(d, d ^ mask) for d in range(ways)])  34.8 us
    dot_general x20, matrix products, contract(): return jnp.einsum(form, left, right, precision=lax.Precision.HIGHEST)  28.7 us
    all_to_all x3, local copies, waits for them, and re-layouts, shards(): lax.all_to_all(stacked, 'ctx', split_axis=3, concat_axis=0, tiled=True)  18.9 us
    all_to_all x1, blocking collectives, shards(): lax.all_to_all(rows_all, 'ctx', split_axis=0, concat_axis=2, tiled=True)  17.4 us
    another operation x1, local copies, waits for them, and re-layouts, shards(): stacked = jnp.stack(turned, axis=1)  15.2 us
  transfers between devices with their start and end apart: 8, of which 4 were waited for; matrix products, arithmetic and copies ran while one was open for 1% of the time, Pallas kernels for 0%

profile of v1, /device:TPU:0, one launch (start us, length us, event | category | flops | bytes accessed | tf_op | source)
XLA Modules:
  0.0 351.6 jit_solution(9312977398790107204)
XLA Ops:
  0.0 3.5 copy.46
  4.0 38.4 %reduce = f32[8192,16]{1,0:T(8,128)} reduce(f32[8192,1,16]{2,1,0:T(1,128)} %bitcast.152, f32[]{:T(128)} %broadcast.483), dimensions={1}, to_apply=%bitcast.134.reduce_sub_computation | reduce | bytes 1048580
  42.4 4.5 %reshape.260 = f32[8,1,16384]{2,1,0:T(1,128)} reshape(f32[8192,16]{1,0:T(8,128)} %reduce) | data formatting | bytes 1048576
  47.0 7.8 %all-to-all-start = ((f32[8,1,16384]{2,1,0:T(1,128)}), f32[8,1,16384]{2,1,0:T(1,128)S(1)}, u32[]{:S(2)}, u32[]{:S(2)}) async-start(f32[8,1,16384]{2,1,0:T(1,128)} %reshape.260), calls=%async_computation | async-start | bytes 1048576 | tf_op jit(solution)/shard_map/all_to_all | solution.py:81
  54.8 1.2 fusion.62
  57.7 11.5 %all-to-all-done = f32[8,1,16384]{2,1,0:T(1,128)S(1)} async-done(((f32[8,1,16384]{2,1,0:T(1,128)}), f32[8,1,16384]{2,1,0:T(1,128)S(1)}, u32[]{:S(2)}, u32[]{:S(2)}) %all-to-all-start) | async-done | bytes 524320 | tf_op jit(solution)/shard_map/all_to_all | solution.py:81
  69.2 1.9 reduce.1
  71.1 10.2 %reshape.261 = f32[8192,1,16]{2,1,0:T(1,128)} reshape(f32[8,16384]{1,0:T(8,128)S(1)} %reduce.1) | data formatting | bytes 1048576
  81.3 3.0 copy.74
  84.3 1.1 convolution_negate_fusion
  85.4 1.3 add_bitcast_fusion
  86.7 0.9 fusion.15
  87.6 1.5 collective-permute-start
  89.4 1.5 collective-permute-start.5
  90.9 0.8 collective-permute-start.4
  91.7 1.6 collective-permute-start.6
  93.3 2.0 collective-permute-start.1
  95.5 1.0 collective-permute-start.2
  96.6 17.9 %collective-permute-done.1 = f32[2,2,16,1024]{3,0,2,1:T(2,128)S(1)} collective-permute-done((f32[2,2,16,1024]{3,0,2,1:T(2,128)S(1)}, f32[2,2,16,1024]{3,0,2,1:T(2,128)S(1)}, u32[]{:S(2)}, u32[]{:S(2)}) %collective-permute-start.1) | collective-permute-done | bytes 262176 | tf_op jit(solution)/shard_map/ppermute | solution.py:19
  114.5 3.3 collective-permute-start.3
  117.9 3.5 %collective-permute-done.2 = f32[2,2,16,1024]{3,0,2,1:T(2,128)S(1)} collective-permute-done((f32[2,2,16,1024]{3,0,2,1:T(2,128)S(1)}, f32[2,2,16,1024]{3,0,2,1:T(2,128)S(1)}, u32[]{:S(2)}, u32[]{:S(2)}) %collective-permute-start.2) | collective-permute-done | bytes 262176 | tf_op jit(solution)/shard_map/ppermute | solution.py:19
  121.5 13.3 %collective-permute-done.3 = f32[2,2,16,1024]{3,0,2,1:T(2,128)S(1)} collective-permute-done((f32[2,2,16,1024]{3,0,2,1:T(2,128)S(1)}, f32[2,2,16,1024]{3,0,2,1:T(2,128)S(1)}, u32[]{:S(2)}, u32[]{:S(2)}) %collective-permute-start.3) | collective-permute-done | bytes 262176 | tf_op jit(solution)/shard_map/ppermute | solution.py:19
  135.3 1.2 fusion.199
  136.5 1.4 stack.46
  137.9 1.5 copy.56
  139.4 1.4 stack.50
  140.8 1.5 copy.59
  142.4 2.4 stack.49
  144.8 2.3 copy.58
  147.2 2.4 stack.47
  149.6 2.4 copy.57
  152.0 2.3 fusion.6
  154.3 1.2 fusion.7
  155.6 1.3 fusion.2
  156.8 1.5 fusion.3
  158.3 1.3 fusion.11
  159.6 1.3 fusion.12
  161.0 1.3 convolution_subtract_fusion.2
  162.3 1.7 multiply_add_fusion.2
  164.0 1.2 fusion.51
  165.2 1.2 fusion.55
  166.3 1.2 convolution_add_fusion.1
  167.5 1.2 convolution_subtract_fusion.1
  168.7 1.2 fusion.14
  169.9 2.6 fusion.13
  172.5 1.2 fusion
  173.8 1.9 copy.62
  175.7 2.1 reshape.248
  177.9 3.4 fusion.1
  181.3 1.8 copy.61
  183.1 1.6 reshape.247
  184.8 1.4 multiply_subtract_fusion
  186.3 15.2 %copy.63 = f32[2,2,16,8192]{2,0,1,3:T(2,128)} copy(f32[2,2,16,8192]{3,2,0,1:T(8,128)S(1)} %pad_maximum_fusion) | data formatting | bytes 4194304 | tf_op jit(solution)/shard_map/stack | solution.py:107
  201.6 24.0 %reshape.262 = f32[8,1,65536]{2,1,0:T(1,128)S(1)} reshape(f32[8192,2,2,16]{3,2,1,0:T(2,128)} %bitcast.149) | data formatting | bytes 4194304
  225.6 51.2 %all_to_all.51 = f32[8,1,65536]{2,1,0:T(1,128)} all-to-all(f32[8,1,65536]{2,1,0:T(1,128)S(1)} %reshape.262), channel_id=1, replica_groups=mesh['ctx'=8,'ch'=4] {'ctx'}, dimensions={0} | all-to-all | bytes 4194304 | tf_op jit(solution)/shard_map/all_to_all | solution.py:108
  276.9 7.2 %reduce.2 = f32[8,65536]{1,0:T(8,128)S(1)} reduce(f32[8,1,65536]{2,1,0:T(1,128)} %all_to_all.51, f32[]{:T(128)} %broadcast.483), dimensions={1}, to_apply=%all_to_all.41.reduce_sub_computation | reduce | bytes 4194308 | tf_op jit(solution)/shard_map/all_to_all | solution.py:108
  284.1 28.5 %reshape.263 = f32[8192,2,2,16]{3,2,1,0:T(2,128)} reshape(f32[8,65536]{1,0:T(8,128)S(1)} %reduce.2) | data formatting | bytes 4194304
  312.5 13.2 %copy.76 = f32[2,2,16,8,1024]{4,3,2,1,0:T(8,128)S(1)} copy(f32[2,2,16,8,1024]{2,0,1,4,3:T(2,128)} %bitcast.150) | data formatting | bytes 4194304 | tf_op jit(solution)/shard_map/all_to_all | solution.py:108
  325.7 3.0 copy.65
  328.7 2.7 all_to_all.44
  331.4 0.6 fusion.5
  332.0 0.6 fusion.4
  333.0 17.4 %all_to_all.52 = f32[8,16,1024]{2,1,0:T(8,128)S(1)} all-to-all(f32[8,16,1024]{2,1,0:T(8,128)S(1)} %copy.66), channel_id=1, replica_groups=mesh['ctx'=8,'ch'=4] {'ctx'}, dimensions={0} | all-to-all | bytes 1048576 | tf_op jit(solution)/shard_map/all_to_all | solution.py:114
  350.5 0.9 add_multiply_fusion
  (42 shorter events, 3.7 us)
Async XLA Ops:
  42.4 13.9 %copy-start.3 = (f32[2,2,16,8192]{3,2,1,0:T(8,128)S(1)}, f32[2,2,16,8192]{3,2,1,0:T(8,128)}, u32[]{:S(2)}) copy-start(f32[2,2,16,8192]{3,2,1,0:T(8,128)} %param.7) | copy-start | bytes 6291460
  47.0 22.2 %all-to-all-start = ((f32[8,1,16384]{2,1,0:T(1,128)}), f32[8,1,16384]{2,1,0:T(1,128)S(1)}, u32[]{:S(2)}, u32[]{:S(2)}) async-start(f32[8,1,16384]{2,1,0:T(1,128)} %reshape.260), calls=%async_computation | async-start | bytes 1048576 | tf_op jit(solution)/shard_map/all_to_all | solution.py:81
  87.6 7.9 %collective-permute-start = (f32[2,2,16,1024]{3,0,2,1:T(2,128)S(1)}, f32[2,2,16,1024]{3,0,2,1:T(2,128)S(1)}, u32[]{:S(2)}, u32[]{:S(2)}) collective-permute-start(f32[2,2,16,1024]{3,0,2,1:T(2,128)S(1)} %get-tuple-element.17), channel_id=1, source_target_pairs={{0,4},{4,0},{8,12},{12,8},{16,20},{20,16},{24,28},{28,24},{1,5},{5... | collective-permute-start | bytes 786440 | tf_op jit(solution)/shard_map/ppermute | solution.py:19
  89.4 45.7 %collective-permute-start.5 = (f32[2,2,16,1024]{3,0,2,1:T(2,128)S(1)}, f32[2,2,16,1024]{3,0,2,1:T(2,128)S(1)}, u32[]{:S(2)}, u32[]{:S(2)}) collective-permute-start(f32[2,2,16,1024]{3,0,2,1:T(2,128)S(1)} %get-tuple-element.21), channel_id=1, source_target_pairs={{0,24},{4,28},{8,16},{12,20},{16,8},{20,12},{24,0},{28,4},{1,25},{... | collective-permute-start | bytes 786440 | tf_op jit(solution)/shard_map/ppermute | solution.py:19
  90.9 44.1 %collective-permute-start.4 = (f32[2,2,16,1024]{3,0,2,1:T(2,128)S(1)}, f32[2,2,16,1024]{3,0,2,1:T(2,128)S(1)}, u32[]{:S(2)}, u32[]{:S(2)}) collective-permute-start(f32[2,2,16,1024]{3,0,2,1:T(2,128)S(1)} %get-tuple-element.22), channel_id=1, source_target_pairs={{0,20},{4,16},{8,28},{12,24},{16,4},{20,0},{24,12},{28,8},{1,21},{... | collective-permute-start | bytes 786440 | tf_op jit(solution)/shard_map/ppermute | solution.py:19
  91.7 43.6 %collective-permute-start.6 = (f32[2,2,16,1024]{3,0,2,1:T(2,128)S(1)}, f32[2,2,16,1024]{3,0,2,1:T(2,128)S(1)}, u32[]{:S(2)}, u32[]{:S(2)}) collective-permute-start(f32[2,2,16,1024]{3,0,2,1:T(2,128)S(1)} %get-tuple-element.15), channel_id=1, source_target_pairs={{0,28},{4,24},{8,20},{12,16},{16,12},{20,8},{24,4},{28,0},{1,29},{... | collective-permute-start | bytes 786440 | tf_op jit(solution)/shard_map/ppermute | solution.py:19
  93.3 21.3 %collective-permute-start.1 = (f32[2,2,16,1024]{3,0,2,1:T(2,128)S(1)}, f32[2,2,16,1024]{3,0,2,1:T(2,128)S(1)}, u32[]{:S(2)}, u32[]{:S(2)}) collective-permute-start(f32[2,2,16,1024]{3,0,2,1:T(2,128)S(1)} %get-tuple-element.18), channel_id=1, source_target_pairs={{0,8},{4,12},{8,0},{12,4},{16,24},{20,28},{24,16},{28,20},{1,9},{5... | collective-permute-start | bytes 786440 | tf_op jit(solution)/shard_map/ppermute | solution.py:19
  95.5 25.9 %collective-permute-start.2 = (f32[2,2,16,1024]{3,0,2,1:T(2,128)S(1)}, f32[2,2,16,1024]{3,0,2,1:T(2,128)S(1)}, u32[]{:S(2)}, u32[]{:S(2)}) collective-permute-start(f32[2,2,16,1024]{3,0,2,1:T(2,128)S(1)} %get-tuple-element.19), channel_id=1, source_target_pairs={{0,12},{4,8},{8,4},{12,0},{16,28},{20,24},{24,20},{28,16},{1,13},{... | collective-permute-start | bytes 786440 | tf_op jit(solution)/shard_map/ppermute | solution.py:19
  114.5 20.4 %collective-permute-start.3 = (f32[2,2,16,1024]{3,0,2,1:T(2,128)S(1)}, f32[2,2,16,1024]{3,0,2,1:T(2,128)S(1)}, u32[]{:S(2)}, u32[]{:S(2)}) collective-permute-start(f32[2,2,16,1024]{3,0,2,1:T(2,128)S(1)} %get-tuple-element.20), channel_id=1, source_target_pairs={{0,16},{4,20},{8,24},{12,28},{16,0},{20,4},{24,8},{28,12},{1,17},{... | collective-permute-start | bytes 786440 | tf_op jit(solution)/shard_map/ppermute | solution.py:19
  152.0 2.3 copy-start.1
  155.6 1.3 copy-start
  332.7 17.8 %copy-start.2 = (f32[16,8192]{1,0:T(8,128)S(1)}, f32[16,8192]{1,0:T(8,128)}, u32[]{:S(2)}) copy-start(f32[16,8192]{1,0:T(8,128)} %param.4) | copy-start | bytes 1572868
  332.7 17.7 %copy-start.4 = (f32[16,8192]{1,0:T(8,128)S(1)}, f32[16,8192]{1,0:T(8,128)}, u32[]{:S(2)}) copy-start(f32[16,8192]{1,0:T(8,128)} %param.5) | copy-start | bytes 1572868
  332.7 17.7 %copy-start.5 = (f32[16]{0:T(128)S(1)}, f32[16]{0:T(128)}, u32[]{:S(2)}) copy-start(f32[16]{0:T(128)} %param.6) | copy-start | bytes 196
